TPU v7x, 32 devices: a whole 2x2x4 slice. The times are simulated.
32 devices in a mesh: lat: 8 (over z, y), lay: 4 (over x, core).
Axes of the slice: x: 2, y: 2, z: 4, core: 2. Of those that a mesh axis runs over, the one named last changes fastest.
Arguments:
- wave_field: float32 [2, 32, 512, 512], P(None, 'lay', 'lat'), may hold values from -6 to 6
- contrast: float32 [32, 512, 512], P('lay', 'lat'), may hold values from 0.1 to 1.5
- layer_of_plane: int32 [32], replicated, may hold values from 0 to 7, never falling along the last dimension, each value on 1 to 8 neighbouring positions
- toeplitz_table: float32 [2, 8, 63], replicated, may hold values from -1 to 1
- hankel_table: float32 [2, 8, 63], replicated, may hold values from -1 to 1
- layer_rates: float32 [8], replicated, may hold values from 0.5 to 1.5
Outputs:
- scattered_field: float32 [2, 32, 512, 512], P(None, 'lay', 'lat')
Inputs may be any that keep to these rules, and one draw needn't show every extreme that they name: `layer_of_plane`: layer numbers never fall from one plane to the next; every layer holds 1 to 8 planes.
All inputs are finite; a program needn't handle non-finite values.
Results may differ from a plain program's by a relative error of at most 0.00007.
Values sent between devices are 32-bit elements; how exact they have to be, the bound alone decides.
A program may use at most 128 MiB of HBM per device.

v0:
```python
import math
import jax
import jax.numpy as jnp
from jax import lax
from jax.sharding import PartitionSpec as P

HIGHEST = lax.Precision.HIGHEST


def signed_of(index, amount):
    return jnp.where(index >= amount // 2, index - amount, index).astype(jnp.float32) / (amount / 2)


def phase_tables(rows, cols, amount, sign):
    index_row = lax.broadcasted_iota(jnp.int32, (rows, cols), 0)
    index_col = lax.broadcasted_iota(jnp.int32, (rows, cols), 1)
    angle = 2.0 * math.pi / amount * (index_row * index_col % amount).astype(jnp.float32)
    return (jnp.cos(angle), sign * jnp.sin(angle))


def complex_apply(real_part, imag_part, cos_table, sin_table, form):
    out_real = jnp.einsum(form, real_part, cos_table, precision=HIGHEST) - jnp.einsum(
        form, imag_part, sin_table, precision=HIGHEST
    )
    out_imag = jnp.einsum(form, real_part, sin_table, precision=HIGHEST) + jnp.einsum(
        form, imag_part, cos_table, precision=HIGHEST
    )
    return (out_real, out_imag)


def fourier_last(real_part, imag_part, sign, factor):
    amount = real_part.shape[-1]
    leading = real_part.shape[:-1]
    first = 1
    for divisor in range(1, math.isqrt(amount) + 1):
        if amount % divisor == 0:
            first = divisor
    second = amount // first
    flat_real = real_part.reshape(-1, second, first)
    flat_imag = imag_part.reshape(-1, second, first)
    cos_second, sin_second = phase_tables(second, second, second, sign)
    section_real, section_imag = complex_apply(
        flat_real, flat_imag, cos_second, sin_second, "pmn,mk->pkn"
    )
    twist_cos, twist_sin = phase_tables(second, first, amount, sign)
    turned_real = section_real * twist_cos - section_imag * twist_sin
    turned_imag = section_real * twist_sin + section_imag * twist_cos
    cos_first, sin_first = phase_tables(first, first, first, sign)
    final_real, final_imag = complex_apply(
        turned_real, turned_imag, cos_first, sin_first, "pkn,nj->pjk"
    )
    final_real = final_real.reshape(leading + (amount,)) * factor
    final_imag = final_imag.reshape(leading + (amount,)) * factor
    return (final_real, final_imag)


def pick_amplitudes(rows, index, width):
    positions = jnp.arange(width, dtype=jnp.int32)
    onehot = (index[:, :, None] == positions[None, None, :]).astype(jnp.float32)
    return jnp.einsum("pan,ain->pai", rows, onehot, precision=HIGHEST)


def body(wave_field, contrast, layer_of_plane, toeplitz_table, hankel_table, layer_rates):
    row_count = wave_field.shape[2]
    width_y = wave_field.shape[3]
    lat_count = lax.axis_size("lat")
    lay_count = lax.axis_size("lay")
    width_x = row_count * lat_count
    ky_band = width_y // lat_count
    table_width = toeplitz_table.shape[-1]
    plane_total = (table_width + 1) // 2
    layer_count = layer_rates.shape[0]
    spec_real, spec_imag = fourier_last(wave_field[0], wave_field[1], -1.0, 1.0)
    along_y = jnp.stack([spec_real, spec_imag], 2)
    freq_x = signed_of(jnp.arange(width_x, dtype=jnp.int32), width_x)
    ky_first = lax.axis_index("lat") * ky_band
    layer_ids = jnp.arange(layer_count, dtype=jnp.int32)

    def couple(z_out, z_in, source, ky_rows):
        onehot = (layer_of_plane[z_out][:, None] == layer_ids[None, :]).astype(jnp.float32)
        rate_out = jnp.dot(onehot, layer_rates, precision=HIGHEST)
        rows_toeplitz = jnp.einsum("al,pln->pan", onehot, toeplitz_table, precision=HIGHEST)
        rows_hankel = jnp.einsum("al,pln->pan", onehot, hankel_table, precision=HIGHEST)
        offset = z_out[:, None] - z_in[None, :]
        plane_sum = z_out[:, None] + z_in[None, :]
        amp_toeplitz = pick_amplitudes(rows_toeplitz, offset + plane_total - 1, table_width)
        amp_hankel = pick_amplitudes(rows_hankel, plane_sum, table_width)
        freq_y = signed_of(ky_rows, width_y)
        steepness = jnp.sqrt(1.0 + freq_y[:, None] ** 2 + freq_x[None, :] ** 2)
        scaled = rate_out[:, None, None, None] * steepness[None, None] / plane_total
        decay_toeplitz = jnp.exp(-scaled * jnp.abs(offset).astype(jnp.float32)[:, :, None, None])
        decay_hankel = jnp.exp(-scaled * (0.5 * plane_sum.astype(jnp.float32))[:, :, None, None])
        kern_real = (
            amp_toeplitz[0][:, :, None, None] * decay_toeplitz
            + amp_hankel[0][:, :, None, None] * decay_hankel
        )
        kern_imag = (
            amp_toeplitz[1][:, :, None, None] * decay_toeplitz
            + amp_hankel[1][:, :, None, None] * decay_hankel
        )
        real_src = source[None, :, 0]
        imag_src = source[None, :, 1]
        out_real = jnp.sum(kern_real * real_src - kern_imag * imag_src, axis=1)
        out_imag = jnp.sum(kern_real * imag_src + kern_imag * real_src, axis=1)
        return jnp.stack([out_real, out_imag], 1)

    narrow = ky_band // lay_count
    narrow_rows = ky_first + lax.axis_index("lay") * narrow + jnp.arange(narrow, dtype=jnp.int32)
    lines_in = lax.all_to_all(along_y, "lat", split_axis=3, concat_axis=1, tiled=True)
    line_real = jnp.transpose(lines_in[:, :, 0], (0, 2, 1))
    line_imag = jnp.transpose(lines_in[:, :, 1], (0, 2, 1))
    out_real, out_imag = fourier_last(line_real, line_imag, -1.0, 1.0)
    spectrum = jnp.stack([out_real, out_imag], 1)
    gathered = lax.all_to_all(spectrum, "lay", split_axis=2, concat_axis=0, tiled=True)
    all_planes = gathered.shape[0]
    every_plane = jnp.arange(all_planes, dtype=jnp.int32)
    block_size = math.gcd(all_planes, 8)

    def one_block(which):
        z_out = which * block_size + jnp.arange(block_size, dtype=jnp.int32)
        return couple(z_out, every_plane, gathered, narrow_rows)

    stacked = lax.map(one_block, jnp.arange(all_planes // block_size, dtype=jnp.int32))
    coupled = stacked.reshape(all_planes, 2, narrow_rows.shape[0], width_x)
    mixed = lax.all_to_all(coupled, "lay", split_axis=0, concat_axis=2, tiled=True)
    out_real, out_imag = fourier_last(mixed[:, 0], mixed[:, 1], 1.0, 1.0 / width_x)
    spatial_x = jnp.transpose(jnp.stack([out_real, out_imag], 1), (0, 3, 1, 2))
    lines = lax.all_to_all(spatial_x, "lat", split_axis=1, concat_axis=3, tiled=True)
    space_real, space_imag = fourier_last(lines[:, :, 0], lines[:, :, 1], 1.0, 1.0 / width_y)
    return jnp.stack([space_real, space_imag], 0) * contrast[None]


def solution(mesh):
    return jax.shard_map(
        body,
        mesh=mesh,
        in_specs=(P(None, "lay", "lat", None), P("lay", "lat", None), P(), P(), P(), P()),
        out_specs=P(None, "lay", "lat", None),
        check_vma=False,
    )
```

profile of v0, /device:TPU:0, one launch (start us, length us, event | category | flops | bytes accessed | tf_op | source)
XLA Modules:
  0.0 411.3 jit_solution(14716647917819366938)
XLA Ops:
  0.1 2.8 fusion.334
  4.1 2.6 fusion.86
  8.3 2.0 copy.197
  10.3 2.2 reshape_squeeze.19
  17.5 2.5 fusion.80
  24.7 2.7 fusion.40
  29.8 3.8 copy_bitcast_fusion.3
  33.6 5.9 %reshape.337 = f32[8,1,65536]{2,1,0:T(1,128)S(1)} reshape(f32[512,2,8,64]{3,2,1,0:T(8,128)} %copy_bitcast_fusion.3) | data formatting | bytes 4194304
  39.6 55.8 %all_to_all.72 = f32[8,1,65536]{2,1,0:T(1,128)} all-to-all(f32[8,1,65536]{2,1,0:T(1,128)S(1)} %reshape.337), channel_id=1, replica_groups=mesh['lat'=8,'lay'=4] {'lat'}, dimensions={0} | all-to-all | bytes 4194304 | tf_op jit(solution)/shard_map/all_to_all | solution.py:109
  95.9 7.1 %reduce = f32[8,65536]{1,0:T(8,128)S(1)} reduce(f32[8,1,65536]{2,1,0:T(1,128)} %all_to_all.72, f32[]{:T(128)} %broadcast.832), dimensions={1}, to_apply=%all_to_all.52.reduce_sub_computation | reduce | bytes 4194308 | tf_op jit(solution)/shard_map/all_to_all | solution.py:109
  103.0 3.6 reshape.338
  106.6 6.6 %copy.340 = f32[8,64,2,8,64]{1,3,4,2,0:T(8,128)} copy(f32[8,64,2,8,64]{1,0,2,4,3:T(8,128)} %bitcast.274) | data formatting | bytes 4194304 | tf_op jit(solution)/shard_map/all_to_all | solution.py:109
  113.3 3.6 all_to_all.55
  118.5 2.0 copy.209
  121.0 2.6 fusion.74
  125.2 2.0 copy.211
  127.2 2.0 reshape.315
  134.2 2.5 fusion.68
  141.6 2.7 fusion.38
  146.7 3.8 pad_maximum_fusion.1
  150.5 4.5 %copy.221 = f32[8,2,64,512]{3,0,1,2:T(8,128)} copy(f32[8,2,64,512]{2,0,3,1:T(8,128)} %pad_maximum_fusion.1) | data formatting | bytes 4194304 | tf_op jit(solution)/shard_map/stack | solution.py:113
  155.0 3.6 all-to-all-start.1
  158.6 25.6 %all-to-all-done.1 = f32[8,2,64,512]{3,0,1,2:T(8,128)S(1)} async-done(((f32[8,2,64,512]{3,0,1,2:T(8,128)}), f32[8,2,64,512]{3,0,1,2:T(8,128)S(1)}, u32[]{:S(2)}, u32[]{:S(2)}) %all-to-all-start.1) | async-done | bytes 2097184 | tf_op jit(solution)/shard_map/all_to_all | solution.py:114
  186.2 46.6 %while.16 = (s32[]{:T(128)}, f32[4,8,2,16,512]{4,3,2,1,0:T(8,128)}, s32[4]{0:T(128)S(1)}, s32[32]{0:T(128)S(1)}, f32[2,8,63]{2,1,0:T(8,128)S(1)}, /*index=5*/f32...) while((s32[]{:T(128)}, f32[4,8,2,16,512]{4,3,2,1,0:T(8,128)}, ...), condition=%wide.region_3.4_spmd.clone.clone, body=%wide.region_0.3_spmd.clone.clone.sunk | while | flops 34766440 | bytes 8512337 | solution.py:123
  190.0 7.1 %subtract_reduce_fusion.2 = (f32[8,16,512]{2,1,0:T(8,128)S(1)}, f32[8,16,512]{2,1,0:T(8,128)S(1)}) fusion(f32[32,16,512]{2,1,0:T(8,128)S(1)} %get-tuple-element.422, f32[8,32]{1,0:T(8,128)S(1)} %bitcast.286, f32[8,32]{1,0:T(8,128)S(1)} %bitcast.288, f32[32,16,512]{2,1,0:T(8,128)S(1)} %get-tuple-element.427, f32[8,32]{1,0:T(8,128)S(1)} %convert_multiply_fusion.2, ...), kind=kLoop, calls=%fused_computation.6.clone.1 | loop fusion | flops 33423360 | bytes 2889728 | tf_op jit(solution)/shard_map/while/body/eval_jaxpr/reduce_sum | solution.py:103
  201.6 7.1 %subtract_reduce_fusion.2 = (f32[8,16,512]{2,1,0:T(8,128)S(1)}, f32[8,16,512]{2,1,0:T(8,128)S(1)}) fusion(f32[32,16,512]{2,1,0:T(8,128)S(1)} %get-tuple-element.422, f32[8,32]{1,0:T(8,128)S(1)} %bitcast.286, f32[8,32]{1,0:T(8,128)S(1)} %bitcast.288, f32[32,16,512]{2,1,0:T(8,128)S(1)} %get-tuple-element.427, f32[8,32]{1,0:T(8,128)S(1)} %convert_multiply_fusion.2, ...), kind=kLoop, calls=%fused_computation.6.clone.1 | loop fusion | flops 33423360 | bytes 2889728 | tf_op jit(solution)/shard_map/while/body/eval_jaxpr/reduce_sum | solution.py:103
  213.3 7.1 %subtract_reduce_fusion.2 = (f32[8,16,512]{2,1,0:T(8,128)S(1)}, f32[8,16,512]{2,1,0:T(8,128)S(1)}) fusion(f32[32,16,512]{2,1,0:T(8,128)S(1)} %get-tuple-element.422, f32[8,32]{1,0:T(8,128)S(1)} %bitcast.286, f32[8,32]{1,0:T(8,128)S(1)} %bitcast.288, f32[32,16,512]{2,1,0:T(8,128)S(1)} %get-tuple-element.427, f32[8,32]{1,0:T(8,128)S(1)} %convert_multiply_fusion.2, ...), kind=kLoop, calls=%fused_computation.6.clone.1 | loop fusion | flops 33423360 | bytes 2889728 | tf_op jit(solution)/shard_map/while/body/eval_jaxpr/reduce_sum | solution.py:103
  224.9 7.1 %subtract_reduce_fusion.2 = (f32[8,16,512]{2,1,0:T(8,128)S(1)}, f32[8,16,512]{2,1,0:T(8,128)S(1)}) fusion(f32[32,16,512]{2,1,0:T(8,128)S(1)} %get-tuple-element.422, f32[8,32]{1,0:T(8,128)S(1)} %bitcast.286, f32[8,32]{1,0:T(8,128)S(1)} %bitcast.288, f32[32,16,512]{2,1,0:T(8,128)S(1)} %get-tuple-element.427, f32[8,32]{1,0:T(8,128)S(1)} %convert_multiply_fusion.2, ...), kind=kLoop, calls=%fused_computation.6.clone.1 | loop fusion | flops 33423360 | bytes 2889728 | tf_op jit(solution)/shard_map/while/body/eval_jaxpr/reduce_sum | solution.py:103
  232.9 4.0 all-to-all-start.2
  236.9 25.6 %all-to-all-done.2 = f32[32,2,16,512]{3,2,1,0:T(8,128)S(1)} async-done(((f32[32,2,16,512]{3,2,1,0:T(8,128)}), f32[32,2,16,512]{3,2,1,0:T(8,128)S(1)}, u32[]{:S(2)}, u32[]{:S(2)}) %all-to-all-start.2) | async-done | bytes 2097184 | tf_op jit(solution)/shard_map/all_to_all | solution.py:125
  265.1 2.6 fusion.62
  271.3 2.2 reshape_squeeze.21
  278.5 2.5 fusion.56
  285.7 2.7 fusion.35
  290.8 3.8 copy_bitcast_fusion.2
  294.6 7.2 %reshape.339 = f32[8,1,65536]{2,1,0:T(1,128)} reshape(f32[512,2,8,64]{3,2,1,0:T(8,128)} %copy_bitcast_fusion.2) | data formatting | bytes 4194304
  301.9 4.9 %all-to-all-start.3 = ((f32[8,1,65536]{2,1,0:T(1,128)}), f32[8,1,65536]{2,1,0:T(1,128)}, u32[]{:S(2)}, u32[]{:S(2)}) async-start(f32[8,1,65536]{2,1,0:T(1,128)} %reshape.339), calls=%async_computation.3 | async-start | bytes 4194304 | tf_op jit(solution)/shard_map/all_to_all | solution.py:128
  306.8 2.0 copy.253
  308.8 46.2 %all-to-all-done.3 = f32[8,1,65536]{2,1,0:T(1,128)} async-done(((f32[8,1,65536]{2,1,0:T(1,128)}), f32[8,1,65536]{2,1,0:T(1,128)}, u32[]{:S(2)}, u32[]{:S(2)}) %all-to-all-start.3) | async-done | bytes 2097184 | tf_op jit(solution)/shard_map/all_to_all | solution.py:128
  354.9 7.1 %reduce.1 = f32[8,65536]{1,0:T(8,128)S(1)} reduce(f32[8,1,65536]{2,1,0:T(1,128)} %all-to-all-done.3, f32[]{:T(128)} %broadcast.832), dimensions={1}, to_apply=%all_to_all.64.reduce_sub_computation | reduce | bytes 4194308 | tf_op jit(solution)/shard_map/all_to_all | solution.py:128
  362.1 3.6 reshape.340
  365.7 6.6 %copy.339 = f32[8,8,64,2,64]{4,1,2,3,0:T(8,128)} copy(f32[8,8,64,2,64]{4,0,3,2,1:T(8,128)} %bitcast.276) | data formatting | bytes 4194304 | tf_op jit(solution)/shard_map/all_to_all | solution.py:128
  372.3 3.6 all_to_all.67
  377.5 2.0 copy.241
  380.0 2.6 fusion.50
  386.2 2.0 reshape_squeeze.23
  402.8 4.5 %maximum_multiply_fusion = f32[2,8,64,512]{2,1,3,0:T(8,128)} fusion(f32[1,8,64,512]{2,1,3,0:T(8,128)} %mul.831, f32[1,8,64,512]{2,1,3,0:T(8,128)} %mul.828, f32[8,64,512]{1,0,2:T(8,128)S(1)} %copy-done.1), kind=kLoop, calls=%fused_computation.56 | loop fusion | flops 1048576 | bytes 5242880 | tf_op jit(solution)/shard_map/mul | solution.py:130
  407.4 3.8 copy.254
  (165 shorter events, 87.1 us)
Async XLA Ops:
  4.1 4.2 %copy-start.9 = (f32[1,8,64,512]{3,2,1,0:T(8,128)S(1)}, f32[1,8,64,512]{3,2,1,0:T(8,128)}, u32[]{:S(2)}) copy-start(f32[1,8,64,512]{3,2,1,0:T(8,128)} %get-tuple-element.352) | copy-start | bytes 3145732
  10.3 2.2 copy-start.2
  121.0 4.2 %copy-start.6 = (f32[8,64,512]{2,1,0:T(8,128)S(1)}, f32[8,64,512]{2,1,0:T(8,128)}, u32[]{:S(2)}) copy-start(f32[8,64,512]{2,1,0:T(8,128)} %get-tuple-element.350) | copy-start | bytes 3145732
  127.2 2.0 copy-start.3
  155.0 29.2 %all-to-all-start.1 = ((f32[8,2,64,512]{3,0,1,2:T(8,128)}), f32[8,2,64,512]{3,0,1,2:T(8,128)S(1)}, u32[]{:S(2)}, u32[]{:S(2)}) async-start(f32[8,2,64,512]{3,0,1,2:T(8,128)} %copy.221), calls=%async_computation.1 | async-start | bytes 4194304 | tf_op jit(solution)/shard_map/all_to_all | solution.py:114
  185.5 0.7 copy-start
  185.5 0.7 copy-start.11
  185.5 0.7 copy-start.12
  185.5 0.7 copy-start.13
  232.9 29.6 %all-to-all-start.2 = ((f32[32,2,16,512]{3,2,1,0:T(8,128)}), f32[32,2,16,512]{3,2,1,0:T(8,128)S(1)}, u32[]{:S(2)}, u32[]{:S(2)}) async-start(f32[32,2,16,512]{3,2,1,0:T(8,128)} %bitcast.22), calls=%async_computation.2 | async-start | bytes 4194304 | tf_op jit(solution)/shard_map/all_to_all | solution.py:125
  265.1 4.2 %copy-start.7 = (f32[8,1,64,512]{3,2,1,0:T(8,128)S(1)}, f32[8,1,64,512]{3,2,1,0:T(8,128)}, u32[]{:S(2)}) copy-start(f32[8,1,64,512]{3,2,1,0:T(8,128)} %get-tuple-element.348) | copy-start | bytes 3145732
  271.3 2.2 copy-start.4
  301.9 4.9 %copy-start.10 = (f32[8,64,512]{2,1,0:T(8,128)S(1)}, f32[8,64,512]{2,1,0:T(8,128)}, u32[]{:S(2)}) copy-start(f32[8,64,512]{2,1,0:T(8,128)} %param.9) | copy-start | bytes 3145732
  301.9 53.1 %all-to-all-start.3 = ((f32[8,1,65536]{2,1,0:T(1,128)}), f32[8,1,65536]{2,1,0:T(1,128)}, u32[]{:S(2)}, u32[]{:S(2)}) async-start(f32[8,1,65536]{2,1,0:T(1,128)} %reshape.339), calls=%async_computation.3 | async-start | bytes 4194304 | tf_op jit(solution)/shard_map/all_to_all | solution.py:128
  380.0 4.2 %copy-start.8 = (f32[8,64,1,512]{3,1,2,0:T(8,128)S(1)}, f32[8,64,1,512]{3,1,2,0:T(8,128)}, u32[]{:S(2)}) copy-start(f32[8,64,1,512]{3,1,2,0:T(8,128)} %get-tuple-element.346) | copy-start | bytes 3145732
  386.2 2.0 copy-start.5
  400.8 2.0 copy-start.1
where the time goes:
time: 417 us; the launch traced here: 411 us
  local copies, waits for them, and re-layouts  113 us (27%)
  waiting for transfers between devices  97.3 us (23%)
  matrix products  65.9 us (16%)
  other arithmetic  63.4 us (15%)
  blocking collectives  55.8 us (13%)
  starting transfers between devices  12.5 us (3%)
    all_to_all x1, blocking collectives, body(): lax.all_to_all(along_y, 'lat', split_axis=3, concat_axis=1, tiled=True)  55.8 us
    all_to_all x1, waiting for transfers between devices, body(): lax.all_to_all(spatial_x, 'lat', split_axis=1, concat_axis=3, tiled=True)  46.2 us
    reduce_sum x4, other arithmetic, couple(): out_real = jnp.sum(kern_real * real_src - kern_imag * imag_src, axis=1)  28.2 us
    all_to_all x1, waiting for transfers between devices, body(): lax.all_to_all(spectrum, 'lay', split_axis=2, concat_axis=0, tiled=True)  25.6 us
    all_to_all x1, waiting for transfers between devices, body(): lax.all_to_all(coupled, 'lay', split_axis=0, concat_axis=2, tiled=True)  25.6 us
    unnamed x34, local copies, waits for them, and re-layouts  23.4 us
    dot_general x8, matrix products, complex_apply(): jnp.einsum(form, real_part, sin_table, precision=HIGHEST)  19.4 us
    dot_general x8, matrix products, complex_apply(): jnp.einsum(form, imag_part, cos_table, precision=HIGHEST)  16.2 us
  transfers between devices with their start and end apart: 3, of which 3 were waited for; matrix products, arithmetic and copies ran while one was open for 1% of the time, Pallas kernels for 0%

commit v1 on v0

--- a/solution.py
+++ b/solution.py
@@ -111,7 +111,9 @@
     line_imag = jnp.transpose(lines_in[:, :, 1], (0, 2, 1))
     out_real, out_imag = fourier_last(line_real, line_imag, -1.0, 1.0)
     spectrum = jnp.stack([out_real, out_imag], 1)
-    gathered = lax.all_to_all(spectrum, "lay", split_axis=2, concat_axis=0, tiled=True)
+    pieces = jnp.split(spectrum, lax.axis_size("lay"), axis=2)
+    received = lax.all_to_all(jnp.stack(pieces), "lay", 0, 0)
+    gathered = jnp.concatenate(received, axis=0)
     all_planes = gathered.shape[0]
     every_plane = jnp.arange(all_planes, dtype=jnp.int32)
     block_size = math.gcd(all_planes, 8)

time: 417 us -> 432 us (1.036)
  local copies, waits for them, and re-layouts: 113 us -> 130 us
    another operation x0 -> x5, local copies, waits for them, and re-layouts: none -> 18.6 us  [body(): received = lax.all_to_all(jnp.stack(pieces), 'lay', 0, 0)]
    another operation x3, local copies, waits for them, and re-layouts: 8.04 us -> 3.67 us  [body(): spectrum = jnp.stack([out_real, out_imag], 1)]
    unnamed x34 -> x37, local copies, waits for them, and re-layouts: 23.4 us -> 27.6 us
  transfers between devices with their start and end apart: 3 -> 3, of which waited for: 3 -> 3; matrix products, arithmetic and copies ran while one was open for 1% -> 0% of each run, Pallas kernels for 0% -> 0%
where the time goes in v1:
time: 432 us; the launch traced here: 427 us
  local copies, waits for them, and re-layouts  130 us (30%)
  waiting for transfers between devices  97.3 us (23%)
  matrix products  65.9 us (15%)
  other arithmetic  61.2 us (14%)
  blocking collectives  55.8 us (13%)
  starting transfers between devices  12.5 us (3%)
    all_to_all x1, blocking collectives, body(): lax.all_to_all(along_y, 'lat', split_axis=3, concat_axis=1, tiled=True)  55.8 us
    all_to_all x1, waiting for transfers between devices, body(): lax.all_to_all(spatial_x, 'lat', split_axis=1, concat_axis=3, tiled=True)  46.1 us
    reduce_sum x4, other arithmetic, couple(): out_real = jnp.sum(kern_real * real_src - kern_imag * imag_src, axis=1)  28.2 us
    unnamed x37, local copies, waits for them, and re-layouts  27.6 us
    all_to_all x1, waiting for transfers between devices, body(): received = lax.all_to_all(jnp.stack(pieces), 'lay', 0, 0)  25.6 us
    all_to_all x1, waiting for transfers between devices, body(): lax.all_to_all(coupled, 'lay', split_axis=0, concat_axis=2, tiled=True)  25.6 us
    another operation x5, local copies, waits for them, and re-layouts, body(): received = lax.all_to_all(jnp.stack(pieces), 'lay', 0, 0)  18.6 us
    dot_general x8, matrix products, complex_apply(): jnp.einsum(form, real_part, sin_table, precision=HIGHEST)  18.4 us
  transfers between devices with their start and end apart: 3, of which 3 were waited for; matrix products, arithmetic and copies ran while one was open for 0% of the time, Pallas kernels for 0%

profile of v1, /device:TPU:0, one launch (start us, length us, event | category | flops | bytes accessed | tf_op | source)
XLA Modules:
  0.0 426.6 jit_solution(14146244545969589838)
XLA Ops:
  0.1 2.8 fusion.334
  4.1 2.6 fusion.86
  10.3 2.2 reshape_squeeze.19
  17.5 2.5 fusion.80
  24.7 2.7 fusion.40
  29.8 3.8 copy_bitcast_fusion.3
  33.6 5.9 %reshape.341 = f32[8,1,65536]{2,1,0:T(1,128)S(1)} reshape(f32[512,2,8,64]{3,2,1,0:T(8,128)} %copy_bitcast_fusion.3) | data formatting | bytes 4194304
  39.6 55.8 %all_to_all.59 = f32[8,1,65536]{2,1,0:T(1,128)} all-to-all(f32[8,1,65536]{2,1,0:T(1,128)S(1)} %reshape.341), channel_id=1, replica_groups=mesh['lat'=8,'lay'=4] {'lat'}, dimensions={0} | all-to-all | bytes 4194304 | tf_op jit(solution)/shard_map/all_to_all | solution.py:109
  95.9 7.2 %reduce = f32[8,65536]{1,0:T(8,128)S(1)} reduce(f32[8,1,65536]{2,1,0:T(1,128)} %all_to_all.59, f32[]{:T(128)} %broadcast.832), dimensions={1}, to_apply=%all_to_all.42.reduce_sub_computation | reduce | bytes 4194308 | tf_op jit(solution)/shard_map/all_to_all | solution.py:109
  103.1 3.6 reshape.342
  106.7 6.6 %copy.339 = f32[8,64,2,8,64]{1,3,4,2,0:T(8,128)} copy(f32[8,64,2,8,64]{1,0,2,4,3:T(8,128)} %bitcast.279) | data formatting | bytes 4194304 | tf_op jit(solution)/shard_map/all_to_all | solution.py:109
  113.3 3.6 all_to_all.45
  118.5 2.0 copy.208
  121.1 2.6 fusion.74
  127.2 2.0 reshape.318
  134.3 2.5 fusion.70
  141.7 2.7 fusion.39
  148.7 7.5 %slice_bitcast_fusion.5 = (f32[1,8,2,16,512]{3,1,4,2,0:T(8,128)}, f32[1,8,2,16,512]{3,1,4,2,0:T(8,128)}, f32[1,8,2,16,512]{3,1,4,2,0:T(8,128)}, f32[1,8,2,16,512]{3,1,4,2,0:T(8,128)}) fusion(f32[8,2,64,512]{2,0,3,1:T(8,128)S(1)} %constant_dynamic-update-slice_fusion), kind=kLoop, calls=%fused_computation.56 | loop fusion | bytes 4194304 | tf_op jit(solution)/shard_map/stack | solution.py:115
  156.1 2.8 copy.220
  158.9 2.8 copy.221
  161.7 2.8 copy.222
  164.5 2.8 copy.223
  168.9 3.6 all-to-all-start.1
  172.5 25.6 %all-to-all-done.1 = f32[4,8,2,16,512]{4,3,2,1,0:T(8,128)S(1)} async-done(((f32[4,8,2,16,512]{4,3,2,1,0:T(8,128)}), f32[4,8,2,16,512]{4,3,2,1,0:T(8,128)S(1)}, u32[]{:S(2)}, u32[]{:S(2)}) %all-to-all-start.1) | async-done | bytes 2097184 | tf_op jit(solution)/shard_map/all_to_all | solution.py:115
  201.3 46.7 %while.16 = (s32[]{:T(128)}, f32[4,8,2,16,512]{4,3,2,1,0:T(8,128)}, s32[4]{0:T(128)S(1)}, s32[32]{0:T(128)S(1)}, f32[2,8,63]{2,1,0:T(8,128)S(1)}, /*index=5*/f32...) while((s32[]{:T(128)}, f32[4,8,2,16,512]{4,3,2,1,0:T(8,128)}, ...), condition=%wide.region_3.4_spmd.clone.clone, body=%wide.region_0.3_spmd.clone.clone.sunk | while | flops 34766440 | bytes 8512337 | solution.py:125
  205.1 7.1 %subtract_reduce_fusion.2 = (f32[8,16,512]{2,1,0:T(8,128)S(1)}, f32[8,16,512]{2,1,0:T(8,128)S(1)}) fusion(f32[32,16,512]{2,1,0:T(8,128)S(1)} %get-tuple-element.426, f32[8,32]{1,0:T(8,128)S(1)} %bitcast.290, f32[8,32]{1,0:T(8,128)S(1)} %bitcast.292, f32[32,16,512]{2,1,0:T(8,128)S(1)} %get-tuple-element.431, f32[8,32]{1,0:T(8,128)S(1)} %convert_multiply_fusion.2, ...), kind=kLoop, calls=%fused_computation.6.clone.1 | loop fusion | flops 33423360 | bytes 2889728 | tf_op jit(solution)/shard_map/while/body/eval_jaxpr/reduce_sum | solution.py:103
  216.8 7.1 %subtract_reduce_fusion.2 = (f32[8,16,512]{2,1,0:T(8,128)S(1)}, f32[8,16,512]{2,1,0:T(8,128)S(1)}) fusion(f32[32,16,512]{2,1,0:T(8,128)S(1)} %get-tuple-element.426, f32[8,32]{1,0:T(8,128)S(1)} %bitcast.290, f32[8,32]{1,0:T(8,128)S(1)} %bitcast.292, f32[32,16,512]{2,1,0:T(8,128)S(1)} %get-tuple-element.431, f32[8,32]{1,0:T(8,128)S(1)} %convert_multiply_fusion.2, ...), kind=kLoop, calls=%fused_computation.6.clone.1 | loop fusion | flops 33423360 | bytes 2889728 | tf_op jit(solution)/shard_map/while/body/eval_jaxpr/reduce_sum | solution.py:103
  228.4 7.1 %subtract_reduce_fusion.2 = (f32[8,16,512]{2,1,0:T(8,128)S(1)}, f32[8,16,512]{2,1,0:T(8,128)S(1)}) fusion(f32[32,16,512]{2,1,0:T(8,128)S(1)} %get-tuple-element.426, f32[8,32]{1,0:T(8,128)S(1)} %bitcast.290, f32[8,32]{1,0:T(8,128)S(1)} %bitcast.292, f32[32,16,512]{2,1,0:T(8,128)S(1)} %get-tuple-element.431, f32[8,32]{1,0:T(8,128)S(1)} %convert_multiply_fusion.2, ...), kind=kLoop, calls=%fused_computation.6.clone.1 | loop fusion | flops 33423360 | bytes 2889728 | tf_op jit(solution)/shard_map/while/body/eval_jaxpr/reduce_sum | solution.py:103
  240.1 7.1 %subtract_reduce_fusion.2 = (f32[8,16,512]{2,1,0:T(8,128)S(1)}, f32[8,16,512]{2,1,0:T(8,128)S(1)}) fusion(f32[32,16,512]{2,1,0:T(8,128)S(1)} %get-tuple-element.426, f32[8,32]{1,0:T(8,128)S(1)} %bitcast.290, f32[8,32]{1,0:T(8,128)S(1)} %bitcast.292, f32[32,16,512]{2,1,0:T(8,128)S(1)} %get-tuple-element.431, f32[8,32]{1,0:T(8,128)S(1)} %convert_multiply_fusion.2, ...), kind=kLoop, calls=%fused_computation.6.clone.1 | loop fusion | flops 33423360 | bytes 2889728 | tf_op jit(solution)/shard_map/while/body/eval_jaxpr/reduce_sum | solution.py:103
  248.0 4.0 all-to-all-start.2
  252.1 25.6 %all-to-all-done.2 = f32[32,2,16,512]{3,2,1,0:T(8,128)S(1)} async-done(((f32[32,2,16,512]{3,2,1,0:T(8,128)}), f32[32,2,16,512]{3,2,1,0:T(8,128)S(1)}, u32[]{:S(2)}, u32[]{:S(2)}) %all-to-all-start.2) | async-done | bytes 2097184 | tf_op jit(solution)/shard_map/all_to_all | solution.py:127
  280.3 2.6 fusion.62
  286.4 2.2 reshape_squeeze.21
  293.6 2.5 fusion.56
  300.9 2.7 fusion.35
  306.0 3.8 copy_bitcast_fusion.2
  309.8 7.2 %reshape.343 = f32[8,1,65536]{2,1,0:T(1,128)} reshape(f32[512,2,8,64]{3,2,1,0:T(8,128)} %copy_bitcast_fusion.2) | data formatting | bytes 4194304
  317.0 4.9 %all-to-all-start.3 = ((f32[8,1,65536]{2,1,0:T(1,128)}), f32[8,1,65536]{2,1,0:T(1,128)}, u32[]{:S(2)}, u32[]{:S(2)}) async-start(f32[8,1,65536]{2,1,0:T(1,128)} %reshape.343), calls=%async_computation.3 | async-start | bytes 4194304 | tf_op jit(solution)/shard_map/all_to_all | solution.py:130
  321.9 2.0 copy.253
  324.0 46.1 %all-to-all-done.3 = f32[8,1,65536]{2,1,0:T(1,128)} async-done(((f32[8,1,65536]{2,1,0:T(1,128)}), f32[8,1,65536]{2,1,0:T(1,128)}, u32[]{:S(2)}, u32[]{:S(2)}) %all-to-all-start.3) | async-done | bytes 2097184 | tf_op jit(solution)/shard_map/all_to_all | solution.py:130
  370.1 7.2 %reduce.1 = f32[8,65536]{1,0:T(8,128)S(1)} reduce(f32[8,1,65536]{2,1,0:T(1,128)} %all-to-all-done.3, f32[]{:T(128)} %broadcast.832), dimensions={1}, to_apply=%all_to_all.51.reduce_sub_computation | reduce | bytes 4194308 | tf_op jit(solution)/shard_map/all_to_all | solution.py:130
  377.3 3.6 reshape.344
  380.9 6.6 %copy.338 = f32[8,8,64,2,64]{4,1,2,3,0:T(8,128)} copy(f32[8,8,64,2,64]{4,0,3,2,1:T(8,128)} %bitcast.281) | data formatting | bytes 4194304 | tf_op jit(solution)/shard_map/all_to_all | solution.py:130
  387.5 3.6 all_to_all.54
  395.2 2.6 fusion.50
  401.4 2.0 reshape_squeeze.23
  418.1 4.5 %maximum_multiply_fusion = f32[2,8,64,512]{2,1,3,0:T(8,128)} fusion(f32[1,8,64,512]{2,1,3,0:T(8,128)} %mul.831, f32[1,8,64,512]{2,1,3,0:T(8,128)} %mul.828, f32[8,64,512]{1,0,2:T(8,128)S(1)} %copy-done.1), kind=kLoop, calls=%fused_computation.59 | loop fusion | flops 1048576 | bytes 5242880 | tf_op jit(solution)/shard_map/mul | solution.py:132
  422.6 3.8 copy.254
  (172 shorter events, 97.7 us)
Async XLA Ops:
  4.1 4.2 copy-start.10
  10.3 2.2 copy-start.3
  121.1 4.2 copy-start.7
  127.2 2.0 copy-start.4
  168.9 29.2 %all-to-all-start.1 = ((f32[4,8,2,16,512]{4,3,2,1,0:T(8,128)}), f32[4,8,2,16,512]{4,3,2,1,0:T(8,128)S(1)}, u32[]{:S(2)}, u32[]{:S(2)}) async-start(f32[4,8,2,16,512]{4,3,2,1,0:T(8,128)} %pad_maximum_fusion.1), calls=%async_computation.1 | async-start | bytes 4194304 | tf_op jit(solution)/shard_map/all_to_all | solution.py:115
  198.1 1.3 copy-start.2
  199.4 1.9 copy-start
  199.4 1.9 copy-start.12
  199.4 1.9 copy-start.13
  199.4 1.9 copy-start.14
  248.0 29.6 %all-to-all-start.2 = ((f32[32,2,16,512]{3,2,1,0:T(8,128)}), f32[32,2,16,512]{3,2,1,0:T(8,128)S(1)}, u32[]{:S(2)}, u32[]{:S(2)}) async-start(f32[32,2,16,512]{3,2,1,0:T(8,128)} %bitcast.23), calls=%async_computation.2 | async-start | bytes 4194304 | tf_op jit(solution)/shard_map/all_to_all | solution.py:127
  280.3 4.2 copy-start.8
  286.4 2.2 copy-start.5
  317.0 4.9 %copy-start.11 = (f32[8,64,512]{2,1,0:T(8,128)S(1)}, f32[8,64,512]{2,1,0:T(8,128)}, u32[]{:S(2)}) copy-start(f32[8,64,512]{2,1,0:T(8,128)} %param.9) | copy-start | bytes 3145732
  317.0 53.1 %all-to-all-start.3 = ((f32[8,1,65536]{2,1,0:T(1,128)}), f32[8,1,65536]{2,1,0:T(1,128)}, u32[]{:S(2)}, u32[]{:S(2)}) async-start(f32[8,1,65536]{2,1,0:T(1,128)} %reshape.343), calls=%async_computation.3 | async-start | bytes 4194304 | tf_op jit(solution)/shard_map/all_to_all | solution.py:130
  395.2 4.2 copy-start.9
  401.4 2.0 copy-start.6
  416.0 2.0 copy-start.1
